TPU v7x, 128 devices: a whole 4x4x4 slice. The times are simulated.
128 devices in a mesh: space: 8 (over z, x_hi), chaos: 16 (over y, x_lo, core).
Axes of the slice: x: 4 (x_hi: 2, x_lo: 2; x = x_hi * 2 + x_lo), y: 4, z: 4, core: 2. Of those that a mesh axis runs over, the one named last changes fastest.
Arguments:
- velocity: float32 [48, 3, 8, 64, 128], P('chaos', None, 'space')
- base_velocity: float32 [48, 3, 8, 64, 128], P('chaos', None, 'space')
- mode_slot: int32 [35], replicated, may hold values from 0 to 47, as said below
- triples: int32 [4096, 3], replicated, may hold values from 0 to 34, as said below
- triple_coef: bfloat16 [4096], replicated, may hold values from -0.29882812 to 0.29882812
Outputs:
- convection: float32 [48, 3, 8, 64, 128], P('chaos', None, 'space')
- next_velocity: float32 [48, 3, 8, 64, 128], P('chaos', None, 'space')
Inputs may be any that keep to these rules, and one draw needn't show every extreme that they name: `mode_slot`: the modes take distinct slots; slots that hold no mode are zero in velocity and base_velocity. `triples`: each triple (i, j, k) of modes is listed at most once.
All inputs are finite; a program needn't handle non-finite values.
Results may differ from a plain program's by a relative error of at most 0.0052.
Values may be sent and summed in bfloat16 or wider, within the bound.
A program may use at most 192 MiB of HBM per device.

v0:
```python
import jax
import jax.numpy as jnp
from jax import lax
from jax.sharding import PartitionSpec as P

SECTION_STEP = 0.5


def extended(block, sides, width):
    for axis, dim in sides:
        count = lax.axis_size(axis)
        forward = [(i, i + 1) for i in range(count - 1)]
        forward.append((count - 1, 0))
        backward = [(target, source) for source, target in forward]
        low = lax.ppermute(
            lax.slice_in_dim(block, block.shape[dim] - width, None, axis=dim), axis, forward
        )
        high = lax.ppermute(lax.slice_in_dim(block, 0, width, axis=dim), axis, backward)
        block = jnp.concatenate([low, block, high], axis=dim)
    return block


def slopes(padded):
    interior = padded[:, :, 1:-1]
    along_x = 0.5 * (padded[:, :, 2:] - padded[:, :, :-2])
    along_y = 0.5 * (jnp.roll(interior, -1, 3) - jnp.roll(interior, 1, 3))
    along_z = 0.5 * (jnp.roll(interior, -1, 4) - jnp.roll(interior, 1, 4))
    return jnp.stack([along_x, along_y, along_z], axis=2)


def pair_table(leading, trailing, weights, leading_count, trailing_count):
    left_hot = (leading[:, None] == jnp.arange(leading_count, dtype=jnp.int32)[None, :]).astype(
        jnp.bfloat16
    ) * weights[:, None]
    right_hot = (trailing[:, None] == jnp.arange(trailing_count, dtype=jnp.int32)[None, :]).astype(
        jnp.bfloat16
    )
    return jnp.einsum("na,nb->ab", left_hot, right_hot, preferred_element_type=jnp.float32).astype(
        jnp.bfloat16
    )


def on_device(velocity, base_velocity, mode_slot, triples, triple_coef):
    slot_dev = velocity.shape[0]
    chaos_count = lax.axis_size("chaos")
    slot_total = slot_dev * chaos_count
    own_index = lax.axis_index("chaos")
    rounded = velocity.astype(jnp.bfloat16)
    slot_i = mode_slot[triples[:, 0]]
    slot_j = mode_slot[triples[:, 1]]
    slot_k = mode_slot[triples[:, 2]]
    padded = extended(rounded, (("space", 2),), 1)
    owned_mask = (slot_j // slot_dev == own_index).astype(jnp.bfloat16)
    coef_table = pair_table(
        slot_k,
        slot_i * slot_dev + slot_j % slot_dev,
        triple_coef * owned_mask,
        slot_total,
        slot_total * slot_dev,
    )
    coef_table = coef_table.reshape(slot_total, slot_total, slot_dev)
    own_slopes = slopes(padded.astype(jnp.float32)).astype(jnp.bfloat16)
    slope_values = own_slopes.astype(jnp.float32)
    moving = lax.all_gather(rounded, "chaos", axis=0, tiled=True)
    weights = jnp.einsum(
        "kij,idxyz->kjdxyz", coef_table, moving, preferred_element_type=jnp.float32
    )
    convection = lax.psum_scatter(
        jnp.einsum("kjdxyz,jcdxyz->kcxyz", weights, slope_values, precision=lax.Precision.HIGHEST),
        "chaos",
        scatter_dimension=0,
        tiled=True,
    )
    next_velocity = base_velocity - SECTION_STEP * convection
    return (convection, next_velocity)


def solution(mesh):
    placed = (
        P("chaos", None, "space", None, None),
        P("chaos", None, "space", None, None),
        P(),
        P(),
        P(),
    )
    return jax.shard_map(
        on_device,
        mesh=mesh,
        in_specs=placed,
        out_specs=(P("chaos", None, "space", None, None), P("chaos", None, "space", None, None)),
        check_vma=False,
    )
```

profile of v0, /device:TPU:1, one launch (start us, length us, event | category | flops | bytes accessed | tf_op | source)
XLA Modules:
  0.0 319.1 jit_solution(2949894726446002743)
XLA Ops:
  7.2 0.0 all-gather.2.cloned.1.call-start
  7.2 1.6 convert_element_type.17
  8.9 0.0 all-gather.2.cloned.1.call-update
  8.9 0.0 reduce-scatter.2.cloned.1.call-start
  8.9 7.1 %collective-permute-start.1 = (bf16[3,3,1,64,128]{4,3,2,1,0:T(8,128)(2,1)}, bf16[3,3,1,64,128]{4,3,2,1,0:T(8,128)(2,1)S(1)}, u32[]{:S(2)}, u32[]{:S(2)}) collective-permute-start(bf16[3,3,1,64,128]{4,3,2,1,0:T(8,128)(2,1)} %convert_element_type.17), channel_id=1, source_target_pairs={{16,0},{32,16},{48,32},{64,48},{80,64},{96,80},{112,96},{0,112},{1... | collective-permute-start | bytes 442376 | tf_op jit(solution)/shard_map/ppermute | solution.py:18
  16.0 0.0 collective-permute-start
  16.0 1.9 fusion.27
  18.0 2.1 fusion.26
  20.1 5.6 %compare_select_fusion.15 = (s32[4096,1]{0,1:T(1,128)S(1)}, s32[4096,1]{0,1:T(1,128)S(1)}, s32[4096,1]{0,1:T(1,128)S(1)}, s32[4096,1]{0,1:T(1,128)S(1)}, s32[4096,1]{0,1:T(1,128)S(1)}, /*index=5*/s32[4096,1]{0,1:T(1,128)S(1)}) fusion(s32[]{:T(128)} %bitcast.28, s32[]{:T(128)} %bitcast.29, s32[]{:T(128)} %bitcast.30, s32[]{:T(128)} %bitcast.31, s32[]{:T(128)} %bitcast.32, ...), kind=kLoop, calls=%fused_computation.124 | loop fusion | flops 184320 | bytes 147484 | tf_op jit(solution)/shard_map/gather | solution.py:51
  25.7 1.4 compare_reduce_fusion.83
  27.0 2.9 compare_reduce_fusion.27
  29.9 17.6 %select_select_fusion.1 = s32[4096]{0:T(1024)S(1)} fusion(pred[4096]{0:T(1024)(128)(4,1)S(1)} %get-tuple-element.33, pred[4096]{0:T(1024)(128)(4,1)S(1)} %get-tuple-element.32, pred[4096]{0:T(1024)(128)(4,1)S(1)} %get-tuple-element.31, pred[4096]{0:T(1024)(128)(4,1)S(1)} %get-tuple-element.30, pred[4096]{0:T(1024)(128)(4,1)S(1)} %get-tuple-element.29, ...), kind=kLoop, calls=%fused_computation.137 | loop fusion | flops 114688 | bytes 147568 | tf_op jit(solution)/shard_map/gather | solution.py:51
  47.5 18.3 %fusion.21 = (bf16[4096]{0:T(1024)(128)(2,1)S(1)}, s32[4096]{0:T(1024)S(1)}) fusion(bf16[4096]{0:T(1024)(128)(2,1)} %param.9, s32[]{:T(128)S(6)} %axis_index.12, pred[4096]{0:T(1024)(128)(4,1)S(1)} %get-tuple-element.147, pred[4096]{0:T(1024)(128)(4,1)S(1)} %get-tuple-element.148, pred[4096]{0:T(1024)(128)(4,1)S(1)} %get-tuple-element.149, ...), kind=kLoop, calls=%fused_computation.140 | loop fusion | flops 155648 | bytes 163956 | tf_op jit(solution)/shard_map/mul | solution.py:57
  65.7 17.6 %fusion.19 = s32[4096]{0:T(1024)S(1)} fusion(pred[4096]{0:T(1024)(128)(4,1)S(1)} %get-tuple-element.89, pred[4096]{0:T(1024)(128)(4,1)S(1)} %get-tuple-element.88, pred[4096]{0:T(1024)(128)(4,1)S(1)} %get-tuple-element.87, pred[4096]{0:T(1024)(128)(4,1)S(1)} %get-tuple-element.86, pred[4096]{0:T(1024)(128)(4,1)S(1)} %get-tuple-element.85, ...), kind=kLoop, calls=%fused_computation.134 | loop fusion | flops 147456 | bytes 163952 | tf_op jit(solution)/shard_map/add | solution.py:56
  83.3 0.6 fusion.5
  83.9 0.1 copy.28
  84.0 0.0 collective-permute-done.1
  84.0 0.0 collective-permute-done
  84.0 0.8 maximum_convert_fusion.1
  84.8 1.0 maximum_convert_fusion
  85.8 0.1 fusion.25
  85.9 0.1 fusion.24
  86.1 0.2 fusion.12
  86.4 0.1 pad_maximum_fusion
  86.5 19.3 %copy.31 = bf16[3,3,3,64,128]{0,1,2,4,3:T(4,128)(2,1)} copy(bf16[3,3,3,64,128]{4,3,2,1,0:T(8,128)(2,1)S(1)} %pad_maximum_fusion) | data formatting | bytes 884736 | tf_op jit(solution)/shard_map/stack | solution.py:28
  105.8 0.0 all-gather.2.cloned.1.call-done
  105.8 8.7 %fusion = f32[48,3,3,64,128]{4,0,3,2,1:T(8,128)} fusion(bf16[48,3,1,64,128]{4,3,2,1,0:T(8,128)(2,1)} %all-gather.2.cloned.1.call-done, bf16[48,48,3,1,1]{0,2,1,4,3:T(4,128)(2,1)S(1)} %bitcast.53), kind=kOutput, calls=%fused_computation.1 | convolution fusion | flops 339738624 | bytes 16528896 | tf_op jit(solution)/shard_map/kij,idxyz->kjdxyz/dot_general | solution.py:65
  114.5 37.1 %copy.32 = f32[48,3,3,64,128]{0,1,2,4,3:T(4,128)} copy(f32[48,3,3,64,128]{4,0,3,2,1:T(8,128)} %fusion) | data formatting | bytes 28311552 | tf_op jit(solution)/shard_map/kij,idxyz->kjdxyz/dot_general | solution.py:65
  151.7 77.3 %convolution_bitcast_fusion = f32[48,3,1,64,128]{0,1,4,3,2:T(4,128)} fusion(bf16[3,3,3,64,128]{0,1,2,4,3:T(4,128)(2,1)} %copy.31, f32[48,3,3,64,128]{0,1,2,4,3:T(4,128)} %copy.32), kind=kOutput, calls=%fused_computation | convolution fusion | flops 127401984 | bytes 19316736 | tf_op jit(solution)/shard_map/kjdxyz,jcdxyz->kcxyz/dot_general | solution.py:69
  229.0 0.0 copy-start
  229.0 11.2 %copy.33 = f32[48,3,1,64,128]{4,3,2,1,0:T(8,128)} copy(f32[48,3,1,64,128]{0,1,4,3,2:T(4,128)} %convolution_bitcast_fusion) | data formatting | bytes 9437184 | tf_op jit(solution)/shard_map/kjdxyz,jcdxyz->kcxyz/transpose | solution.py:69
  240.1 0.0 reduce-scatter.2.cloned.1.call-update
  240.2 70.4 %reduce-scatter.2.cloned.1.call-done = f32[3,3,1,64,128]{4,3,2,1,0:T(8,128)} async-done(((f32[48,3,1,64,128]{4,3,2,1,0:T(8,128)}), f32[3,3,1,64,128]{4,3,2,1,0:T(8,128)}) %reduce-scatter.2.cloned.1.call-update) | async-done | bytes 294928 | tf_op jit(solution)/shard_map/reduce_scatter | solution.py:68
  310.6 0.0 copy-done
  310.6 1.7 multiply_subtract_fusion
  (3 shorter events, 0.1 us)
Async XLA Ops:
  7.2 98.6 %all-gather.2.cloned.1.call-start = ((), (), s32[]{:S(2)}) async-start(), calls=%async_computation.1 | async-start | bytes 2506752 | tf_op jit(solution)/shard_map/all_gather | solution.py:64
  8.9 301.7 %reduce-scatter.2.cloned.1.call-start = ((), (), s32[]{:S(2)}) async-start(), calls=%async_computation.2 | async-start | bytes 5013504 | tf_op jit(solution)/shard_map/reduce_scatter | solution.py:68
  8.9 75.1 %collective-permute-start.1 = (bf16[3,3,1,64,128]{4,3,2,1,0:T(8,128)(2,1)}, bf16[3,3,1,64,128]{4,3,2,1,0:T(8,128)(2,1)S(1)}, u32[]{:S(2)}, u32[]{:S(2)}) collective-permute-start(bf16[3,3,1,64,128]{4,3,2,1,0:T(8,128)(2,1)} %convert_element_type.17), channel_id=1, source_target_pairs={{16,0},{32,16},{48,32},{64,48},{80,64},{96,80},{112,96},{0,112},{1... | collective-permute-start | bytes 442376 | tf_op jit(solution)/shard_map/ppermute | solution.py:18
  16.0 68.0 %collective-permute-start = (bf16[3,3,1,64,128]{4,3,2,1,0:T(8,128)(2,1)}, bf16[3,3,1,64,128]{4,3,2,1,0:T(8,128)(2,1)S(1)}, u32[]{:S(2)}, u32[]{:S(2)}) collective-permute-start(bf16[3,3,1,64,128]{4,3,2,1,0:T(8,128)(2,1)} %convert_element_type.17), channel_id=1, source_target_pairs={{0,16},{16,32},{32,48},{48,64},{64,80},{80,96},{96,112},{112,0},{1... | collective-permute-start | bytes 442376 | tf_op jit(solution)/shard_map/ppermute | solution.py:15
  229.0 81.6 %copy-start = (f32[3,3,1,64,128]{4,3,2,1,0:T(8,128)S(1)}, f32[3,3,1,64,128]{4,3,2,1,0:T(8,128)}, u32[]{:S(2)}) copy-start(f32[3,3,1,64,128]{4,3,2,1,0:T(8,128)} %param.6) | copy-start | bytes 884740
Sparse Core Ops, SparseCore 0:
  10.3 38.0 all-gather.1
  240.3 70.2 reduce-scatter.1
where the time goes:
time: 323 us; the launch traced here: 319 us
  matrix products  86.6 us (27%)
  local copies, waits for them, and re-layouts  72.1 us (22%)
  waiting for transfers between devices  70.5 us (22%)
  other arithmetic  68.6 us (21%)
  between operations  14.2 us (4%)
  starting transfers between devices  7.2 us (2%)
    dot_general x1, matrix products, on_device(): jnp.einsum('kjdxyz,jcdxyz->kcxyz', weights, slope_values, precision=lax.P...  77.3 us
    reduce_scatter x1, waiting for transfers between devices, on_device(): lax.psum_scatter(jnp.einsum('kjdxyz,jcdxyz->kcxyz', weights, slope_values...  70.4 us
    dot_general x1, local copies, waits for them, and re-layouts, on_device(): jnp.einsum('kij,idxyz->kjdxyz', coef_table, moving, preferred_element_typ...  37.1 us
    gather x3, other arithmetic, on_device(): slot_k = mode_slot[triples[:, 2]]  24.5 us
    another operation x1, local copies, waits for them, and re-layouts, slopes(): return jnp.stack([along_x, along_y, along_z], axis=2)  19.3 us
    mul x1, other arithmetic, on_device(): triple_coef * owned_mask  18.3 us
    add x1, other arithmetic, on_device(): slot_i * slot_dev + slot_j % slot_dev  17.6 us
    transpose x1, local copies, waits for them, and re-layouts, on_device(): jnp.einsum('kjdxyz,jcdxyz->kcxyz', weights, slope_values, precision=lax.P...  11.2 us
  transfers between devices with their start and end apart: 4, of which 1 were waited for; matrix products, arithmetic and copies ran while one was open for 28% of the time, Pallas kernels for 0%

commit v1 on v0

v1 whole, which is shorter than its diff:
```python
import functools

import jax
import jax.numpy as jnp
from jax import lax
from jax.experimental import pallas as pl
from jax.experimental.pallas import tpu as pltpu
from jax.sharding import PartitionSpec as P

MESH = pl.DeviceIdType.MESH
SECTION_STEP = 0.5

MODES = 35
SLOT_DEV = 3
CHAOS = 16
GROUP = 32
MODE_PAD = 48
OUT_PAD = 40
JH = 9
LANES = 128
WIDE = 3 * LANES
TABLE_ROWS = JH * OUT_PAD
TABLE_CHUNK = 1024

F32 = jnp.float32
BF16 = jnp.bfloat16


def iota(shape, dim):
    return lax.broadcasted_iota(jnp.int32, shape, dim)


def ring_place(x_hi, chaos):
    y = chaos // 4
    x = 2 * x_hi + (chaos // 2) % 2
    return 2 * (4 * y + x + (y % 2) * (3 - 2 * x)) + chaos % 2


def ring_device(place):
    chip = place // 2
    y = chip // 4
    q = chip % 4
    x = q + (y % 2) * (3 - 2 * q)
    return x // 2, 4 * y + 2 * (x % 2) + place % 2


def dot(a, b, contract=((1,), (0,))):
    return lax.dot_general(a, b, (contract, ((), ())), preferred_element_type=F32)


def kernel(
    space_count,
    velocity_ref,
    slot_ref,
    triples_ref,
    coef_ref,
    out_ref,
    vel,
    send,
    recv,
    field,
    halo_x,
    halo_y,
    table,
    slope,
    weights,
    back,
    home,
    load_sem,
    own_sem,
    send_sem,
    recv_sem,
    halo_send_sem,
    halo_recv_sem,
    back_own_sem,
    back_send_sem,
    back_recv_sem,
):
    space = lax.axis_index("space")
    chaos = lax.axis_index("chaos")
    plane_pair = space // 2
    x_hi = space % 2
    place = ring_place(x_hi, chaos)
    pairs = space_count // 2
    z_up = lax.rem(plane_pair + 1, pairs)
    z_down = lax.rem(plane_pair + pairs - 1, pairs)

    def in_group(other):
        other_hi, other_chaos = ring_device(other)
        return other_hi, other_chaos, (2 * plane_pair + other_hi, other_chaos)

    load = pltpu.make_async_copy(velocity_ref, vel, load_sem)
    load.start()

    barrier = pltpu.get_barrier_semaphore()

    def greet(step, carry):
        _, _, device = in_group(lax.rem(place + step, GROUP))
        pl.semaphore_signal(barrier, inc=1, device_id=device, device_id_type=MESH)
        return carry

    lax.fori_loop(1, GROUP, greet, 0)
    for z in (z_up, z_down):
        pl.semaphore_signal(barrier, inc=1, device_id=(2 * z + x_hi, chaos), device_id_type=MESH)

    row = iota((GROUP * 8, SLOT_DEV * 64), 0)
    col = iota((GROUP * 8, SLOT_DEV * 64), 1)
    spread = (col == ((row // 2) % 4) * 64 + (row // 8) * 2 + row % 2).astype(F32).astype(BF16)
    load.wait()
    values = jnp.concatenate(
        [
            jnp.concatenate([vel[a, d, 0] for d in range(3)], axis=1).astype(BF16)
            for a in range(SLOT_DEV)
        ],
        axis=0,
    )
    send[...] = dot(spread, values).reshape(GROUP, 8, WIDE).astype(BF16)

    pl.semaphore_wait(barrier, GROUP + 1)

    own = pltpu.make_async_copy(send.at[place], recv.at[CHAOS * x_hi + chaos], own_sem)
    own.start()

    def scatter(step, carry):
        other = lax.rem(place + step, GROUP)
        _, _, device = in_group(other)
        pltpu.make_async_remote_copy(
            src_ref=send.at[other],
            dst_ref=recv.at[CHAOS * x_hi + chaos],
            send_sem=send_sem,
            recv_sem=recv_sem,
            device_id=device,
            device_id_type=MESH,
        ).start()
        return carry

    lax.fori_loop(1, GROUP, scatter, 0)

    def add_triples(chunk, carry):
        at = pl.ds(pl.multiple_of(chunk * TABLE_CHUNK, TABLE_CHUNK), TABLE_CHUNK)
        mode_i = triples_ref[0:1, at]
        mode_j = triples_ref[1:2, at]
        mode_k = triples_ref[2:3, at]
        coef = coef_ref[0:1, at].astype(F32)
        high = (mode_j // 4) * OUT_PAD + mode_k
        low = (mode_j % 4) * 64 + mode_i
        left = jnp.where(iota((TABLE_ROWS, TABLE_CHUNK), 0) == high, coef, 0.0).astype(BF16)
        right = jnp.where(iota((256, TABLE_CHUNK), 0) == low, 1.0, 0.0).astype(BF16)
        part = dot(left, right, ((1,), (1,)))
        weights[0:TABLE_ROWS, 0:256] += part
        return carry

    weights[0:TABLE_ROWS, 0:256] = jnp.zeros((TABLE_ROWS, 256), F32)
    lax.fori_loop(0, 4096 // TABLE_CHUNK, add_triples, 0)
    table[...] = weights[0:TABLE_ROWS, 0:256].astype(BF16)

    slots = jnp.broadcast_to(slot_ref[...], (CHAOS * 8, LANES))
    source = iota((CHAOS * 8, LANES), 0)
    hit = (slots == (source // 8) * SLOT_DEV + (source // 2) % 4) & ((source // 2) % 4 < SLOT_DEV)
    hit = hit & (iota((CHAOS * 8, LANES), 1) < MODES)
    gather = [
        jnp.where(hit & (source % 2 == r), 1.0, 0.0)[:, :MODE_PAD] for r in range(2)
    ]
    gather = jnp.concatenate(gather, axis=1)
    to_modes = jnp.concatenate([gather, jnp.zeros((CHAOS * 8, 32), F32)], axis=1).T[: 2 * MODE_PAD]
    to_modes = to_modes.astype(BF16)
    to_slots = gather.astype(BF16)

    own.wait()
    rest = pl.ds(0, GROUP - 1)
    pltpu.make_async_copy(recv.at[rest], recv.at[rest], recv_sem).wait()

    for p in range(2):
        got = recv[p * CHAOS : (p + 1) * CHAOS].astype(F32).reshape(CHAOS * 8, WIDE).astype(BF16)
        modes = dot(to_modes, got).astype(BF16)
        for r in range(2):
            field[p, r] = modes[r * MODE_PAD : (r + 1) * MODE_PAD]

    _, _, ahead = in_group(lax.rem(place + 1, GROUP))
    _, _, behind = in_group(lax.rem(place + GROUP - 1, GROUP))
    below = (2 * z_down + x_hi, chaos)
    above = (2 * z_up + x_hi, chaos)
    halos = [
        (field.at[0], halo_x.at[1], below),
        (field.at[1], halo_x.at[0], above),
        (field.at[:, 0], halo_y.at[1], behind),
        (field.at[:, 1], halo_y.at[0], ahead),
    ]
    halo_copies = [
        pltpu.make_async_remote_copy(
            src_ref=source_ref,
            dst_ref=target_ref,
            send_sem=halo_send_sem.at[n],
            recv_sem=halo_recv_sem.at[n],
            device_id=device,
            device_id_type=MESH,
        )
        for n, (source_ref, target_ref, device) in enumerate(halos)
    ]
    for copy in halo_copies:
        copy.start()

    def put_slope(d, p, r, high, low):
        value = (0.5 * (high - low)).astype(BF16).astype(F32)
        for c in range(3):
            slope[p, r, 3 * d + c] = value[:, c * LANES : (c + 1) * LANES]

    for p in range(2):
        for r in range(2):
            for c in range(3):
                at = slice(c * LANES, (c + 1) * LANES)
                here = field[p, r, :, at].astype(F32)
                slope[p, r, 6 + c] = (
                    (0.5 * (pltpu.roll(here, LANES - 1, 1) - pltpu.roll(here, 1, 1)))
                    .astype(BF16)
                    .astype(F32)
                )

    for copy in halo_copies:
        copy.wait_recv()

    for r in range(2):
        first = field[0, r].astype(F32)
        second = field[1, r].astype(F32)
        put_slope(0, 0, r, second, halo_x[0, r].astype(F32))
        put_slope(0, 1, r, halo_x[1, r].astype(F32), first)
    for p in range(2):
        first = field[p, 0].astype(F32)
        second = field[p, 1].astype(F32)
        put_slope(1, p, 0, second, halo_y[0, p].astype(F32))
        put_slope(1, p, 1, halo_y[1, p].astype(F32), first)

    blank = jnp.zeros((64 - MODE_PAD, WIDE), BF16)
    none = jnp.zeros((64, WIDE), BF16)
    for p in range(2):
        parts = []
        for r in range(2):
            modes = jnp.concatenate([field[p, r], blank], axis=0)
            for jl in range(4):
                pair = [modes, none] if jl % 2 == 0 else [none, modes]
                weights[jl * TABLE_ROWS : (jl + 1) * TABLE_ROWS] = dot(
                    table[:, (jl // 2) * 128 : (jl // 2 + 1) * 128], jnp.concatenate(pair, axis=0)
                )

            def add_mode(jh, sums):
                for jl in range(4):
                    j = jh * 4 + jl
                    rows = pl.ds(pl.multiple_of(jl * TABLE_ROWS + jh * OUT_PAD, 8), OUT_PAD)
                    new = list(sums)
                    for d in range(3):
                        weight = weights[rows, d * LANES : (d + 1) * LANES]
                        for c in range(3):
                            value = slope[p, r, 3 * d + c, pl.ds(j, OUT_PAD, stride=0)]
                            new[c] = new[c] + weight * value
                    sums = tuple(new)
                return sums

            zero = jnp.zeros((OUT_PAD, LANES), F32)
            sums = lax.fori_loop(0, JH, add_mode, (zero, zero, zero))
            part = jnp.concatenate(sums, axis=1)
            parts.append(jnp.concatenate([part, jnp.zeros((8, WIDE), F32)], axis=0).astype(BF16))
        result = jnp.concatenate(parts, axis=0)
        back[p] = dot(to_slots, result).reshape(CHAOS, 8, WIDE).astype(BF16)

        def give(step, carry):
            target = lax.rem(chaos + step, CHAOS)

            @pl.when((target != chaos) | (x_hi != p))
            def _():
                pltpu.make_async_remote_copy(
                    src_ref=back.at[p, target],
                    dst_ref=home.at[place],
                    send_sem=back_send_sem,
                    recv_sem=back_recv_sem,
                    device_id=(2 * plane_pair + p, target),
                    device_id_type=MESH,
                ).start()

            return carry

        lax.fori_loop(0, CHAOS, give, 0)

    own_back = pltpu.make_async_copy(back.at[x_hi, chaos], home.at[place], back_own_sem)
    own_back.start()

    row = iota((SLOT_DEV * 64, GROUP * 8), 0)
    col = iota((SLOT_DEV * 64, GROUP * 8), 1)
    collect = (row == ((col // 2) % 4) * 64 + (col // 8) * 2 + col % 2).astype(F32).astype(BF16)

    own_back.wait()
    pltpu.make_async_copy(home.at[rest], home.at[rest], back_recv_sem).wait()
    got = home[...].astype(F32).reshape(GROUP * 8, WIDE).astype(BF16)
    result = dot(collect, got)
    for a in range(SLOT_DEV):
        for c in range(3):
            out_ref[a, c, 0] = result[a * 64 : (a + 1) * 64, c * LANES : (c + 1) * LANES].astype(BF16)

    pltpu.make_async_copy(send.at[rest], send.at[rest], send_sem).wait()
    for copy in halo_copies:
        copy.wait_send()
    pltpu.make_async_copy(home.at[rest], home.at[rest], back_send_sem).wait()


def on_device(velocity, base_velocity, mode_slot, triples, triple_coef):
    space_count = lax.axis_size("space")
    slots = jnp.pad(mode_slot, (0, LANES - MODES), constant_values=-1).reshape(1, LANES)
    in_vmem = pl.BlockSpec(memory_space=pltpu.VMEM)
    dma = pltpu.SemaphoreType.DMA
    convection = pl.pallas_call(
        functools.partial(kernel, space_count),
        out_shape=jax.ShapeDtypeStruct(velocity.shape, BF16),
        in_specs=[pl.BlockSpec(memory_space=pl.ANY), in_vmem, in_vmem, in_vmem],
        out_specs=in_vmem,
        scratch_shapes=[
            pltpu.VMEM(velocity.shape, F32),
            pltpu.VMEM((GROUP, 8, WIDE), BF16),
            pltpu.VMEM((GROUP, 8, WIDE), BF16),
            pltpu.VMEM((2, 2, MODE_PAD, WIDE), BF16),
            pltpu.VMEM((2, 2, MODE_PAD, WIDE), BF16),
            pltpu.VMEM((2, 2, MODE_PAD, WIDE), BF16),
            pltpu.VMEM((TABLE_ROWS, 256), BF16),
            pltpu.VMEM((2, 2, 9, MODE_PAD, LANES), F32),
            pltpu.VMEM((4 * TABLE_ROWS, WIDE), F32),
            pltpu.VMEM((2, CHAOS, 8, WIDE), BF16),
            pltpu.VMEM((GROUP, 8, WIDE), BF16),
            dma,
            dma,
            dma,
            dma,
            dma((4,)),
            dma((4,)),
            dma,
            dma,
            dma,
        ],
        compiler_params=pltpu.CompilerParams(
            collective_id=0, has_side_effects=True, vmem_limit_bytes=32 * 1024 * 1024
        ),
    )(velocity, slots, triples.T, triple_coef.reshape(1, -1)).astype(F32)
    next_velocity = base_velocity - SECTION_STEP * convection
    return (convection, next_velocity)


def solution(mesh):
    placed = P("chaos", None, "space", None, None)
    return jax.shard_map(
        on_device,
        mesh=mesh,
        in_specs=(placed, placed, P(), P(), P()),
        out_specs=(placed, placed),
        check_vma=False,
    )
```

time: 323 us -> 32.4 us (0.10); the launches traced: 319 us -> 32.2 us
  matrix products: 86.6 us -> 0 us
  waiting for transfers between devices: 70.5 us -> 0 us
  local copies, waits for them, and re-layouts: 72.1 us -> 3.16 us
  other arithmetic: 68.6 us -> 0.87 us
  Pallas kernels: 0 us -> 27.5 us
  between operations: 14.2 us -> 0.67 us
  starting transfers between devices: 7.2 us -> 0 us
    dot_general x3 -> x0, matrix products: 86.6 us -> none  [the longest x1 77.3 us: on_device(): jnp.einsum('kjdxyz,jcdxyz->kcxyz', weights, slope_values, precision=lax.P...]
    reduce_scatter x1 -> x0, waiting for transfers between devices: 70.4 us -> none  [on_device(): lax.psum_scatter(jnp.einsum('kjdxyz,jcdxyz->kcxyz', weights, slope_values...]
    dot_general x1 -> x0, local copies, waits for them, and re-layouts: 37.1 us -> none  [on_device(): jnp.einsum('kij,idxyz->kjdxyz', coef_table, moving, preferred_element_typ...]
    pallas_call x0 -> x1, Pallas kernels: none -> 27.5 us  [on_device(): pl.pallas_call(functools.partial(kernel, space_count), out_shape=jax.Shap...]
    gather x4 -> x0, other arithmetic: 27.4 us -> none  [the longest x3 24.5 us: on_device(): slot_k = mode_slot[triples[:, 2]]]
    another operation x1 -> x0, local copies, waits for them, and re-layouts: 19.3 us -> none  [slopes(): return jnp.stack([along_x, along_y, along_z], axis=2)]
    mul x1 -> x0, other arithmetic: 18.3 us -> none  [on_device(): triple_coef * owned_mask]
    add x1 -> x0, other arithmetic: 17.6 us -> none  [on_device(): slot_i * slot_dev + slot_j % slot_dev]
  transfers between devices with their start and end apart: 4 -> 0, of which waited for: 1 -> 0; matrix products, arithmetic and copies ran while one was open for 28% -> 0% of each run, Pallas kernels for 0% -> 0%
where the time goes in v1:
time: 32.4 us; the launch traced here: 32.2 us
  Pallas kernels  27.5 us (85%)
  local copies, waits for them, and re-layouts  3.16 us (10%)
  other arithmetic  0.87 us (3%)
  between operations  0.67 us (2%)
    pallas_call x1, Pallas kernels, on_device(): pl.pallas_call(functools.partial(kernel, space_count), out_shape=jax.Shap...  27.5 us
    unnamed x8, local copies, waits for them, and re-layouts  2.45 us
    sub x1, other arithmetic, on_device(): next_velocity = base_velocity - SECTION_STEP * convection  0.87 us
    reshape x1, local copies, waits for them, and re-layouts, on_device(): triple_coef.reshape(1, -1)  0.71 us

profile of v1, /device:TPU:1, one launch (start us, length us, event | category | flops | bytes accessed | tf_op | source)
XLA Modules:
  0.0 32.2 jit_solution(6108608810017127396)
XLA Ops:
  0.6 0.0 copy-start.3
  0.6 0.6 %copy-done.3 = s32[35]{0:T(128)S(1)} copy-done((s32[35]{0:T(128)S(1)}, s32[35]{0:T(128)}, u32[]{:S(2)}) %copy-start.3) | copy-done | bytes 164
  1.3 0.7 %reshape.11.coef_ref = bf16[1,4096]{1,0:T(2,128)(2,1)S(1)} reshape(bf16[4096]{0:T(1024)(128)(2,1)} %param.9) | data formatting | bytes 16384 | tf_op jit(solution)/shard_map/reshape | solution.py:339
  2.0 0.0 copy-start
  2.0 1.0 %copy-done = f32[3,3,1,64,128]{4,3,2,1,0:T(8,128)S(1)} copy-done((f32[3,3,1,64,128]{4,3,2,1,0:T(8,128)S(1)}, f32[3,3,1,64,128]{4,3,2,1,0:T(8,128)}, u32[]{:S(2)}) %copy-start) | copy-done | bytes 294936
  3.0 0.0 copy-start.1
  3.0 0.8 %copy-done.1 = s32[4096,3]{0,1:T(4,128)S(1)} copy-done((s32[4096,3]{0,1:T(4,128)S(1)}, s32[4096,3]{0,1:T(4,128)}, u32[]{:S(2)}) %copy-start.1) | copy-done | bytes 49176
  3.8 0.0 copy-start.2
  3.8 27.5 %shard_map.68 = bf16[3,3,1,64,128]{4,3,2,1,0:T(8,128)(2,1)S(1)} custom-call(f32[3,3,1,64,128]{4,3,2,1,0:T(8,128)S(1)} %copy-done, s32[1,128]{1,0:T(1,128)S(1)} %pad_bitcast_fusion.slot_ref, s32[3,4096]{1,0:T(4,128)S(1)} %bitcast.3, bf16[1,4096]{1,0:T(2,128)(2,1)S(1)} %reshape.11.coef_ref), custom_call_target="tpu_custom_call" | custom-call | tf_op jit(solution)/shard_map/pallas_call | solution.py:309
  31.3 0.0 copy-done.2
  31.3 0.9 %multiply_subtract_fusion = (f32[3,3,1,64,128]{4,3,2,1,0:T(8,128)}, f32[3,3,1,64,128]{4,3,2,1,0:T(8,128)}) fusion(f32[3,3,1,64,128]{4,3,2,1,0:T(8,128)S(1)} %copy-done.2, bf16[3,3,1,64,128]{4,3,2,1,0:T(8,128)(2,1)S(1)} %shard_map.68), kind=kLoop, calls=%fused_computation | loop fusion | flops 221184 | bytes 1032192 | tf_op jit(solution)/shard_map/sub | solution.py:340
  (1 shorter events, 0.0 us)
Async XLA Ops:
  0.6 0.7 %copy-start.3 = (s32[35]{0:T(128)S(1)}, s32[35]{0:T(128)}, u32[]{:S(2)}) copy-start(s32[35]{0:T(128)} %param.7) | copy-start | bytes 424
  2.0 1.0 %copy-start = (f32[3,3,1,64,128]{4,3,2,1,0:T(8,128)S(1)}, f32[3,3,1,64,128]{4,3,2,1,0:T(8,128)}, u32[]{:S(2)}) copy-start(f32[3,3,1,64,128]{4,3,2,1,0:T(8,128)} %velocity_ref.1) | copy-start | bytes 884740
  3.0 0.8 %copy-start.1 = (s32[4096,3]{0,1:T(4,128)S(1)}, s32[4096,3]{0,1:T(4,128)}, u32[]{:S(2)}) copy-start(s32[4096,3]{0,1:T(4,128)} %param.8) | copy-start | bytes 147460
  3.8 27.5 %copy-start.2 = (f32[3,3,1,64,128]{4,3,2,1,0:T(8,128)S(1)}, f32[3,3,1,64,128]{4,3,2,1,0:T(8,128)}, u32[]{:S(2)}) copy-start(f32[3,3,1,64,128]{4,3,2,1,0:T(8,128)} %param.6) | copy-start | bytes 884740

commit v2 on v1

v2 whole, which is shorter than its diff:
```python
import functools

import jax
import jax.numpy as jnp
from jax import lax
from jax.experimental import pallas as pl
from jax.experimental.pallas import tpu as pltpu
from jax.sharding import PartitionSpec as P

MESH = pl.DeviceIdType.MESH
SECTION_STEP = 0.5

MODES = 35
SLOT_DEV = 3
CHAOS = 16
GROUP = 32
MODE_PAD = 48
OUT_PAD = 40
JH = 9
LANES = 128
WIDE = 3 * LANES
TABLE_ROWS = JH * OUT_PAD
TABLE_CHUNK = 1024
TRIPLES = 4096

F32 = jnp.float32
BF16 = jnp.bfloat16


def iota(shape, dim):
    return lax.broadcasted_iota(jnp.int32, shape, dim)


def ring_place(x_hi, chaos):
    y = chaos // 4
    x = 2 * x_hi + (chaos // 2) % 2
    return 2 * (4 * y + x + (y % 2) * (3 - 2 * x)) + chaos % 2


def ring_device(place):
    chip = place // 2
    y = chip // 4
    q = chip % 4
    x = q + (y % 2) * (3 - 2 * q)
    return x // 2, 4 * y + 2 * (x % 2) + place % 2


def place_of(member):
    hi = member >> 4
    y = (member >> 2) & 3
    x = 2 * hi + ((member >> 1) & 1)
    return 2 * (4 * y + x + (y & 1) * (3 - 2 * x)) + (member & 1)


def dot(a, b, contract=((1,), (0,))):
    return lax.dot_general(a, b, (contract, ((), ())), preferred_element_type=F32)


def kernel(
    space_count,
    velocity_ref,
    slot_ref,
    triples_ref,
    coef_ref,
    out_ref,
    vel,
    slot_row,
    triples,
    coefs,
    send,
    recv,
    field,
    edge,
    halo_x,
    halo_y,
    sums,
    table,
    slope,
    weights,
    partial,
    back,
    home,
    load_sem,
    own_sem,
    send_sem,
    recv_sem,
    halo_send_sem,
    halo_recv_sem,
    back_own_sem,
    back_send_sem,
    back_recv_sem,
):
    space = lax.axis_index("space")
    chaos = lax.axis_index("chaos")
    plane_pair = space // 2
    x_hi = space % 2
    me = CHAOS * x_hi + chaos
    pairs = space_count // 2
    z_up = lax.rem(plane_pair + 1, pairs)
    z_down = lax.rem(plane_pair + pairs - 1, pairs)

    loads = [
        pltpu.make_async_copy(source_ref, target_ref, load_sem.at[n])
        for n, (source_ref, target_ref) in enumerate(
            [
                (velocity_ref, vel),
                (triples_ref, triples),
                (coef_ref, coefs),
                (slot_ref, slot_row),
            ]
        )
    ]
    for load in loads:
        load.start()

    far = 1 - x_hi
    planes = (far, x_hi)

    def each_member(turn, act):
        def go(step, carry):
            act(planes[turn], lax.rem(chaos + step, CHAOS))
            return carry

        lax.fori_loop(turn, CHAOS, go, 0, unroll=4 if turn == 0 else 5)

    barrier = pltpu.get_barrier_semaphore()

    def greet(hi, other):
        pl.semaphore_signal(
            barrier, inc=1, device_id=(2 * plane_pair + hi, other), device_id_type=MESH
        )

    for turn in range(2):
        each_member(turn, greet)
    for z in (z_up, z_down):
        pl.semaphore_signal(barrier, inc=1, device_id=(2 * z + x_hi, chaos), device_id_type=MESH)

    row = iota((GROUP * 8, LANES), 0)
    source_row = ((row >> 1) & 3) * 64 + place_of(row >> 3) * 2 + (row & 1)
    lane = iota((GROUP * 8, LANES), 1)
    spread = jnp.concatenate(
        [
            jnp.where(source_row == lane, 1.0, 0.0),
            jnp.where(source_row == lane + LANES, 1.0, 0.0)[:, :64],
        ],
        axis=1,
    ).astype(BF16)
    loads[0].wait()
    values = jnp.concatenate(
        [
            jnp.concatenate([vel[a, d, 0] for d in range(3)], axis=1).astype(BF16)
            for a in range(SLOT_DEV)
        ],
        axis=0,
    )
    send[...] = dot(spread, values).reshape(GROUP, 8, WIDE).astype(BF16)

    pl.semaphore_wait(barrier, GROUP + 1)

    def give(hi, other):
        pltpu.make_async_remote_copy(
            src_ref=send.at[CHAOS * hi + other],
            dst_ref=recv.at[me],
            send_sem=send_sem,
            recv_sem=recv_sem,
            device_id=(2 * plane_pair + hi, other),
            device_id_type=MESH,
        ).start()

    for turn in range(2):
        each_member(turn, give)
    own = pltpu.make_async_copy(send.at[me], recv.at[me], own_sem)
    own.start()

    for load in loads[1:]:
        load.wait()

    sums[...] = jnp.zeros((TABLE_ROWS, 256), F32)

    def add_triples(chunk, carry):
        at = pl.ds(pl.multiple_of(chunk * TABLE_CHUNK, TABLE_CHUNK), TABLE_CHUNK)
        mode_i = triples[0:1, at]
        mode_j = triples[1:2, at]
        mode_k = triples[2:3, at]
        eight = coefs[chunk].astype(F32)
        coef = jnp.concatenate([eight[q : q + 1] for q in range(8)], axis=1)
        high = (mode_j >> 2) * OUT_PAD + mode_k
        low = (mode_j & 3) * 64 + mode_i
        left = jnp.where(iota((TABLE_ROWS, TABLE_CHUNK), 0) == high, coef, 0.0).astype(BF16)
        right = jnp.where(iota((256, TABLE_CHUNK), 0) == low, 1.0, 0.0).astype(BF16)
        sums[...] += dot(left, right, ((1,), (1,)))
        return carry

    lax.fori_loop(0, TRIPLES // TABLE_CHUNK, add_triples, 0)
    table[...] = sums[...].astype(BF16)

    source = iota((CHAOS * 8, MODES), 0)
    slot_of = (source >> 3) * SLOT_DEV + ((source >> 1) & 3)
    hit = (slot_row[...] == slot_of) & (((source >> 1) & 3) < SLOT_DEV)
    gap = jnp.zeros((CHAOS * 8, MODE_PAD - MODES), F32)
    gather = []
    for r in range(2):
        gather += [jnp.where(hit & ((source & 1) == r), 1.0, 0.0), gap]
    gather = jnp.concatenate(gather + [jnp.zeros((CHAOS * 8, 32), F32)], axis=1)
    to_modes = gather.T[: 2 * MODE_PAD].astype(BF16)
    to_slots = gather[:, : 2 * MODE_PAD].astype(BF16)

    own.wait()
    rest = pl.ds(0, GROUP - 1)
    pltpu.make_async_copy(recv.at[rest], recv.at[rest], recv_sem).wait()

    for p in range(2):
        got = recv[p * CHAOS : (p + 1) * CHAOS].astype(F32).reshape(CHAOS * 8, WIDE).astype(BF16)
        modes = dot(to_modes, got)
        for r in range(2):
            rows = modes[r * MODE_PAD : (r + 1) * MODE_PAD]
            field[p, r] = rows.astype(BF16)
            edge[p, r] = rows[:OUT_PAD].reshape(OUT_PAD // 8, 8, WIDE).astype(BF16)

    place = ring_place(x_hi, chaos)
    next_hi, next_chaos = ring_device(lax.rem(place + 1, GROUP))
    last_hi, last_chaos = ring_device(lax.rem(place + GROUP - 1, GROUP))
    ahead = (2 * plane_pair + next_hi, next_chaos)
    behind = (2 * plane_pair + last_hi, last_chaos)
    halo_copies = []
    for p in planes:
        up = p * z_down + (1 - p) * z_up
        for r in range(2):
            for kind, source_ref, target_ref, device in (
                (0, edge.at[1 - p, r], halo_x.at[p, r], (2 * up + x_hi, chaos)),
                (1, edge.at[p, 1 - r], halo_y.at[p, r], ahead if r == 0 else behind),
            ):
                halo_copies.append(
                    pltpu.make_async_remote_copy(
                        src_ref=source_ref,
                        dst_ref=target_ref,
                        send_sem=halo_send_sem.at[4 * kind + 2 * p + r],
                        recv_sem=halo_recv_sem.at[4 * kind + 2 * p + r],
                        device_id=device,
                        device_id_type=MESH,
                    )
                )
                halo_copies[-1].start()

    def weigh(n, carry):
        p, r = n >> 1, n & 1
        modes = jnp.concatenate([field[p, r], jnp.zeros((64 - MODE_PAD, WIDE), BF16)], axis=0)
        none = jnp.zeros((64, WIDE), BF16)
        for jl in range(4):
            pair = [modes, none] if jl % 2 == 0 else [none, modes]
            weights[n, jl * TABLE_ROWS : (jl + 1) * TABLE_ROWS] = dot(
                table[:, (jl // 2) * 128 : (jl // 2 + 1) * 128], jnp.concatenate(pair, axis=0)
            )
        for c in range(3):
            here = field[p, r, :, c * LANES : (c + 1) * LANES].astype(F32)[:OUT_PAD]
            turn = pltpu.roll(here, LANES - 1, 1) - pltpu.roll(here, 1, 1)
            slope[n, 6 + c] = (0.5 * turn).astype(BF16).astype(F32)
        return carry

    lax.fori_loop(0, 4, weigh, 0)

    def add_terms(n, directions, start):
        def add_mode(jh, totals):
            totals = list(totals)
            for jl in range(4):
                rows = pl.ds(pl.multiple_of(jl * TABLE_ROWS + jh * OUT_PAD, 8), OUT_PAD)
                for d in directions:
                    weight = weights[n, rows, d * LANES : (d + 1) * LANES]
                    for c in range(3):
                        value = slope[n, 3 * d + c, pl.ds(jh * 4 + jl, OUT_PAD, stride=0)]
                        totals[c] = totals[c] + weight * value
            return tuple(totals)

        return lax.fori_loop(0, JH, add_mode, start)

    def add_z(n, carry):
        zero = jnp.zeros((OUT_PAD, LANES), F32)
        for c, total in enumerate(add_terms(n, (2,), (zero, zero, zero))):
            partial[n, c] = total
        return carry

    lax.fori_loop(0, 4, add_z, 0)

    def values_of(ref, p, r):
        return ref[p, r].astype(F32).reshape(OUT_PAD, WIDE)

    def put_slope(d, n, value):
        value = value.astype(BF16).astype(F32)
        for c in range(3):
            slope[n, 3 * d + c] = value[:, c * LANES : (c + 1) * LANES]

    for turn, p in enumerate(planes):
        half = 0.5 - p.astype(F32)
        rows = []
        for r in range(2):
            n = 2 * p + r
            for copy in halo_copies[4 * turn + 2 * r : 4 * turn + 2 * r + 2]:
                copy.wait_recv()
            put_slope(0, n, half * (values_of(edge, 1 - p, r) - values_of(halo_x, p, r)))
            turned = values_of(edge, p, 1 - r) - values_of(halo_y, p, r)
            put_slope(1, n, (0.5 - r) * turned)
            totals = add_terms(n, (0, 1), tuple(partial[n, c] for c in range(3)))
            rows += [jnp.concatenate(totals, axis=1), jnp.zeros((8, WIDE), F32)]
        result = jnp.concatenate(rows, axis=0).astype(BF16)
        back[p] = dot(to_slots, result).reshape(CHAOS, 8, WIDE).astype(BF16)

        def give_back(hi, other):
            pltpu.make_async_remote_copy(
                src_ref=back.at[hi, other],
                dst_ref=home.at[me],
                send_sem=back_send_sem,
                recv_sem=back_recv_sem,
                device_id=(2 * plane_pair + hi, other),
                device_id_type=MESH,
            ).start()

        each_member(turn, give_back)

    own_back = pltpu.make_async_copy(back.at[x_hi, chaos], home.at[me], back_own_sem)
    own_back.start()

    row = iota((SLOT_DEV * 64, LANES), 0)
    lane = iota((SLOT_DEV * 64, LANES), 1)
    collect = []
    for half in range(2):
        col = lane + half * LANES
        collect.append(
            jnp.where(row == ((col >> 1) & 3) * 64 + place_of(col >> 3) * 2 + (col & 1), 1.0, 0.0)
        )
    collect = jnp.concatenate(collect, axis=1).astype(BF16)

    own_back.wait()
    pltpu.make_async_copy(home.at[rest], home.at[rest], back_recv_sem).wait()
    got = home[...].astype(F32).reshape(GROUP * 8, WIDE).astype(BF16)
    result = dot(collect, got)
    for a in range(SLOT_DEV):
        for c in range(3):
            out_ref[a, c, 0] = result[a * 64 : (a + 1) * 64, c * LANES : (c + 1) * LANES].astype(BF16)

    pltpu.make_async_copy(send.at[rest], send.at[rest], send_sem).wait()
    for copy in halo_copies:
        copy.wait_send()
    pltpu.make_async_copy(home.at[rest], home.at[rest], back_send_sem).wait()


def on_device(velocity, base_velocity, mode_slot, triples, triple_coef):
    space_count = lax.axis_size("space")
    in_hbm = pl.BlockSpec(memory_space=pltpu.HBM)
    operands = (
        velocity,
        mode_slot.reshape(1, MODES),
        triples.T,
        triple_coef.reshape(TRIPLES // TABLE_CHUNK, 8, LANES),
    )
    dma = pltpu.SemaphoreType.DMA
    convection = pl.pallas_call(
        functools.partial(kernel, space_count),
        out_shape=jax.ShapeDtypeStruct(velocity.shape, BF16),
        in_specs=[in_hbm] * 4,
        out_specs=pl.BlockSpec(memory_space=pltpu.VMEM),
        scratch_shapes=[
            pltpu.VMEM(velocity.shape, F32),
            pltpu.VMEM((1, MODES), jnp.int32),
            pltpu.VMEM((3, TRIPLES), jnp.int32),
            pltpu.VMEM((TRIPLES // TABLE_CHUNK, 8, LANES), BF16),
            pltpu.VMEM((GROUP, 8, WIDE), BF16),
            pltpu.VMEM((GROUP, 8, WIDE), BF16),
            pltpu.VMEM((2, 2, MODE_PAD, WIDE), BF16),
            pltpu.VMEM((2, 2, OUT_PAD // 8, 8, WIDE), BF16),
            pltpu.VMEM((2, 2, OUT_PAD // 8, 8, WIDE), BF16),
            pltpu.VMEM((2, 2, OUT_PAD // 8, 8, WIDE), BF16),
            pltpu.VMEM((TABLE_ROWS, 256), F32),
            pltpu.VMEM((TABLE_ROWS, 256), BF16),
            pltpu.VMEM((4, 9, OUT_PAD, LANES), F32),
            pltpu.VMEM((4, 4 * TABLE_ROWS, WIDE), F32),
            pltpu.VMEM((4, 3, OUT_PAD, LANES), F32),
            pltpu.VMEM((2, CHAOS, 8, WIDE), BF16),
            pltpu.VMEM((GROUP, 8, WIDE), BF16),
            dma((4,)),
            dma,
            dma,
            dma,
            dma((8,)),
            dma((8,)),
            dma,
            dma,
            dma,
        ],
        compiler_params=pltpu.CompilerParams(
            collective_id=0, has_side_effects=True, vmem_limit_bytes=40 * 1024 * 1024
        ),
    )(*(pltpu.with_memory_space_constraint(value, pltpu.HBM) for value in operands)).astype(F32)
    next_velocity = base_velocity - SECTION_STEP * convection
    return (convection, next_velocity)


def solution(mesh):
    placed = P("chaos", None, "space", None, None)
    return jax.shard_map(
        on_device,
        mesh=mesh,
        in_specs=(placed, placed, P(), P(), P()),
        out_specs=(placed, placed),
        check_vma=False,
    )
```

time: 32.4 us -> 26.6 us (0.82)
  local copies, waits for them, and re-layouts: 3.16 us -> 0.01 us
  Pallas kernels: 27.5 us -> 25 us
    pallas_call x1, Pallas kernels: 27.5 us -> 25 us  [on_device(): pl.pallas_call(functools.partial(kernel, space_count), out_shape=jax.Shap...]
    unnamed x8 -> x2, local copies, waits for them, and re-layouts: 2.45 us -> 0.01 us
    reshape x2 -> x0, local copies, waits for them, and re-layouts: 0.71 us -> none  [the longest x1 0.71 us: on_device(): triple_coef.reshape(1, -1)]
where the time goes in v2:
time: 26.6 us; the launch traced here: 26.5 us
  Pallas kernels  25 us (94%)
  other arithmetic  0.87 us (3%)
  between operations  0.65 us (2%)
    pallas_call x1, Pallas kernels, on_device(): pl.pallas_call(functools.partial(kernel, space_count), out_shape=jax.Shap...  25 us
    sub x1, other arithmetic, on_device(): next_velocity = base_velocity - SECTION_STEP * convection  0.87 us

profile of v2, /device:TPU:1, one launch (start us, length us, event | category | flops | bytes accessed | tf_op | source)
XLA Modules:
  0.0 26.5 jit_solution(4454323083837814286)
XLA Ops:
  0.6 0.0 copy-start
  0.6 25.0 %shard_map.68 = bf16[3,3,1,64,128]{4,3,2,1,0:T(8,128)(2,1)S(1)} custom-call(f32[3,3,1,64,128]{4,3,2,1,0:T(8,128)} %velocity_ref.1, s32[1,35]{1,0:T(1,128)} %bitcast.5, s32[3,4096]{1,0:T(4,128)} %bitcast.3, bf16[4,8,128]{2,1,0:T(8,128)(2,1)} %bitcast.4), custom_call_target="tpu_custom_call" | custom-call | tf_op jit(solution)/shard_map/pallas_call | solution.py:356
  25.6 0.0 copy-done
  25.6 0.9 %multiply_subtract_fusion = (f32[3,3,1,64,128]{4,3,2,1,0:T(8,128)}, f32[3,3,1,64,128]{4,3,2,1,0:T(8,128)}) fusion(f32[3,3,1,64,128]{4,3,2,1,0:T(8,128)S(1)} %copy-done, bf16[3,3,1,64,128]{4,3,2,1,0:T(8,128)(2,1)S(1)} %shard_map.68), kind=kLoop, calls=%fused_computation | loop fusion | flops 221184 | bytes 1032192 | tf_op jit(solution)/shard_map/sub | solution.py:393
Async XLA Ops:
  0.6 25.0 %copy-start = (f32[3,3,1,64,128]{4,3,2,1,0:T(8,128)S(1)}, f32[3,3,1,64,128]{4,3,2,1,0:T(8,128)}, u32[]{:S(2)}) copy-start(f32[3,3,1,64,128]{4,3,2,1,0:T(8,128)} %param.6) | copy-start | bytes 884740

commit v3 on v2

--- a/solution.py
+++ b/solution.py
@@ -71,7 +71,7 @@
     recv,
     field,
     edge,
-    halo_x,
+    outer,
     halo_y,
     sums,
     table,
@@ -84,6 +84,9 @@
     own_sem,
     send_sem,
     recv_sem,
+    ready_sem,
+    outer_send_sem,
+    outer_recv_sem,
     halo_send_sem,
     halo_recv_sem,
     back_own_sem,
@@ -121,7 +124,8 @@
             act(planes[turn], lax.rem(chaos + step, CHAOS))
             return carry
 
-        lax.fori_loop(turn, CHAOS, go, 0, unroll=4 if turn == 0 else 5)
+        lax.fori_loop(CHAOS // 2, CHAOS, go, 0, unroll=4)
+        lax.fori_loop(turn, CHAOS // 2, go, 0, unroll=4 if turn == 0 else 7)
 
     barrier = pltpu.get_barrier_semaphore()
 
@@ -132,8 +136,9 @@
 
     for turn in range(2):
         each_member(turn, greet)
-    for z in (z_up, z_down):
-        pl.semaphore_signal(barrier, inc=1, device_id=(2 * z + x_hi, chaos), device_id_type=MESH)
+    toward = x_hi * z_up + (1 - x_hi) * z_down
+    away = x_hi * z_down + (1 - x_hi) * z_up
+    pl.semaphore_signal(barrier, inc=1, device_id=(2 * toward + x_hi, chaos), device_id_type=MESH)
 
     row = iota((GROUP * 8, LANES), 0)
     source_row = ((row >> 1) & 3) * 64 + place_of(row >> 3) * 2 + (row & 1)
@@ -155,7 +160,30 @@
     )
     send[...] = dot(spread, values).reshape(GROUP, 8, WIDE).astype(BF16)
 
-    pl.semaphore_wait(barrier, GROUP + 1)
+    def give_halos():
+        pl.semaphore_wait(ready_sem, 1)
+        for hi in planes:
+
+            def give_halo(step, carry):
+                other = lax.rem(chaos + step, CHAOS)
+                pltpu.make_async_remote_copy(
+                    src_ref=send.at[CHAOS * hi + other],
+                    dst_ref=outer.at[far, chaos],
+                    send_sem=outer_send_sem,
+                    recv_sem=outer_recv_sem.at[far],
+                    device_id=(2 * toward + hi, other),
+                    device_id_type=MESH,
+                ).start()
+                return carry
+
+            lax.fori_loop(0, CHAOS, give_halo, 0, unroll=4)
+
+    pl.semaphore_wait(barrier, GROUP)
+    pl.semaphore_signal(ready_sem, inc=1, device_id=(2 * away + x_hi, chaos), device_id_type=MESH)
+
+    @pl.when(toward == 0)
+    def _():
+        give_halos()
 
     def give(hi, other):
         pltpu.make_async_remote_copy(
@@ -171,6 +199,10 @@
         each_member(turn, give)
     own = pltpu.make_async_copy(send.at[me], recv.at[me], own_sem)
     own.start()
+
+    @pl.when(toward != 0)
+    def _():
+        give_halos()
 
     for load in loads[1:]:
         load.wait()
@@ -224,23 +256,18 @@
     behind = (2 * plane_pair + last_hi, last_chaos)
     halo_copies = []
     for p in planes:
-        up = p * z_down + (1 - p) * z_up
         for r in range(2):
-            for kind, source_ref, target_ref, device in (
-                (0, edge.at[1 - p, r], halo_x.at[p, r], (2 * up + x_hi, chaos)),
-                (1, edge.at[p, 1 - r], halo_y.at[p, r], ahead if r == 0 else behind),
-            ):
-                halo_copies.append(
-                    pltpu.make_async_remote_copy(
-                        src_ref=source_ref,
-                        dst_ref=target_ref,
-                        send_sem=halo_send_sem.at[4 * kind + 2 * p + r],
-                        recv_sem=halo_recv_sem.at[4 * kind + 2 * p + r],
-                        device_id=device,
-                        device_id_type=MESH,
-                    )
+            halo_copies.append(
+                pltpu.make_async_remote_copy(
+                    src_ref=edge.at[p, 1 - r],
+                    dst_ref=halo_y.at[p, r],
+                    send_sem=halo_send_sem.at[2 * p + r],
+                    recv_sem=halo_recv_sem.at[2 * p + r],
+                    device_id=ahead if r == 0 else behind,
+                    device_id_type=MESH,
                 )
-                halo_copies[-1].start()
+            )
+            halo_copies[-1].start()
 
     def weigh(n, carry):
         p, r = n >> 1, n & 1
@@ -291,12 +318,14 @@
 
     for turn, p in enumerate(planes):
         half = 0.5 - p.astype(F32)
+        pltpu.make_async_copy(outer.at[p], outer.at[p], outer_recv_sem.at[p]).wait()
+        beyond = dot(to_modes, outer[p].astype(F32).reshape(CHAOS * 8, WIDE).astype(BF16))
         rows = []
         for r in range(2):
             n = 2 * p + r
-            for copy in halo_copies[4 * turn + 2 * r : 4 * turn + 2 * r + 2]:
-                copy.wait_recv()
-            put_slope(0, n, half * (values_of(edge, 1 - p, r) - values_of(halo_x, p, r)))
+            halo_copies[2 * turn + r].wait_recv()
+            outside = beyond[r * MODE_PAD : r * MODE_PAD + OUT_PAD]
+            put_slope(0, n, half * (values_of(edge, 1 - p, r) - outside))
             turned = values_of(edge, p, 1 - r) - values_of(halo_y, p, r)
             put_slope(1, n, (0.5 - r) * turned)
             totals = add_terms(n, (0, 1), tuple(partial[n, c] for c in range(3)))
@@ -338,6 +367,7 @@
             out_ref[a, c, 0] = result[a * 64 : (a + 1) * 64, c * LANES : (c + 1) * LANES].astype(BF16)
 
     pltpu.make_async_copy(send.at[rest], send.at[rest], send_sem).wait()
+    pltpu.make_async_copy(send, send, outer_send_sem).wait()
     for copy in halo_copies:
         copy.wait_send()
     pltpu.make_async_copy(home.at[rest], home.at[rest], back_send_sem).wait()
@@ -367,7 +397,7 @@
             pltpu.VMEM((GROUP, 8, WIDE), BF16),
             pltpu.VMEM((2, 2, MODE_PAD, WIDE), BF16),
             pltpu.VMEM((2, 2, OUT_PAD // 8, 8, WIDE), BF16),
-            pltpu.VMEM((2, 2, OUT_PAD // 8, 8, WIDE), BF16),
+            pltpu.VMEM((2, CHAOS, 8, WIDE), BF16),
             pltpu.VMEM((2, 2, OUT_PAD // 8, 8, WIDE), BF16),
             pltpu.VMEM((TABLE_ROWS, 256), F32),
             pltpu.VMEM((TABLE_ROWS, 256), BF16),
@@ -380,8 +410,11 @@
             dma,
             dma,
             dma,
-            dma((8,)),
-            dma((8,)),
+            pltpu.SemaphoreType.REGULAR,
+            dma,
+            dma((2,)),
+            dma((4,)),
+            dma((4,)),
             dma,
             dma,
             dma,

time: 26.6 us -> 25.5 us (0.959)
  Pallas kernels: 25 us -> 23.9 us
    pallas_call x1, Pallas kernels: 25 us -> 23.9 us  [on_device(): pl.pallas_call(functools.partial(kernel, space_count), out_shape=jax.Shap...]
where the time goes in v3:
time: 25.5 us; the launch traced here: 25.4 us
  Pallas kernels  23.9 us (94%)
  other arithmetic  0.87 us (3%)
  between operations  0.65 us (3%)
    pallas_call x1, Pallas kernels, on_device(): pl.pallas_call(functools.partial(kernel, space_count), out_shape=jax.Shap...  23.9 us
    sub x1, other arithmetic, on_device(): next_velocity = base_velocity - SECTION_STEP * convection  0.87 us

profile of v3, /device:TPU:1, one launch (start us, length us, event | category | flops | bytes accessed | tf_op | source)
XLA Modules:
  0.0 25.4 jit_solution(2294500719841811143)
XLA Ops:
  0.6 0.0 copy-start
  0.6 23.9 %shard_map.68 = bf16[3,3,1,64,128]{4,3,2,1,0:T(8,128)(2,1)S(1)} custom-call(f32[3,3,1,64,128]{4,3,2,1,0:T(8,128)} %velocity_ref.1, s32[1,35]{1,0:T(1,128)} %bitcast.5, s32[3,4096]{1,0:T(4,128)} %bitcast.3, bf16[4,8,128]{2,1,0:T(8,128)(2,1)} %bitcast.4), custom_call_target="tpu_custom_call" | custom-call | tf_op jit(solution)/shard_map/pallas_call | solution.py:386
  24.5 0.0 copy-done
  24.5 0.9 %multiply_subtract_fusion = (f32[3,3,1,64,128]{4,3,2,1,0:T(8,128)}, f32[3,3,1,64,128]{4,3,2,1,0:T(8,128)}) fusion(f32[3,3,1,64,128]{4,3,2,1,0:T(8,128)S(1)} %copy-done, bf16[3,3,1,64,128]{4,3,2,1,0:T(8,128)(2,1)S(1)} %shard_map.68), kind=kLoop, calls=%fused_computation | loop fusion | flops 221184 | bytes 1032192 | tf_op jit(solution)/shard_map/sub | solution.py:426
Async XLA Ops:
  0.6 23.9 %copy-start = (f32[3,3,1,64,128]{4,3,2,1,0:T(8,128)S(1)}, f32[3,3,1,64,128]{4,3,2,1,0:T(8,128)}, u32[]{:S(2)}) copy-start(f32[3,3,1,64,128]{4,3,2,1,0:T(8,128)} %param.6) | copy-start | bytes 884740

commit v4 on v3

--- a/solution.py
+++ b/solution.py
@@ -19,6 +19,7 @@
 JH = 9
 LANES = 128
 WIDE = 3 * LANES
+USED = pl.ds(0, 2 * SLOT_DEV)
 TABLE_ROWS = JH * OUT_PAD
 TABLE_CHUNK = 1024
 TRIPLES = 4096
@@ -127,6 +128,10 @@
         lax.fori_loop(CHAOS // 2, CHAOS, go, 0, unroll=4)
         lax.fori_loop(turn, CHAOS // 2, go, 0, unroll=4 if turn == 0 else 7)
 
+    recv[...] = jnp.zeros(recv.shape, BF16)
+    outer[...] = jnp.zeros(outer.shape, BF16)
+    home[...] = jnp.zeros(home.shape, BF16)
+
     barrier = pltpu.get_barrier_semaphore()
 
     def greet(hi, other):
@@ -167,8 +172,8 @@
             def give_halo(step, carry):
                 other = lax.rem(chaos + step, CHAOS)
                 pltpu.make_async_remote_copy(
-                    src_ref=send.at[CHAOS * hi + other],
-                    dst_ref=outer.at[far, chaos],
+                    src_ref=send.at[CHAOS * hi + other, USED],
+                    dst_ref=outer.at[far, chaos, USED],
                     send_sem=outer_send_sem,
                     recv_sem=outer_recv_sem.at[far],
                     device_id=(2 * toward + hi, other),
@@ -187,8 +192,8 @@
 
     def give(hi, other):
         pltpu.make_async_remote_copy(
-            src_ref=send.at[CHAOS * hi + other],
-            dst_ref=recv.at[me],
+            src_ref=send.at[CHAOS * hi + other, USED],
+            dst_ref=recv.at[me, USED],
             send_sem=send_sem,
             recv_sem=recv_sem,
             device_id=(2 * plane_pair + hi, other),
@@ -239,7 +244,7 @@
 
     own.wait()
     rest = pl.ds(0, GROUP - 1)
-    pltpu.make_async_copy(recv.at[rest], recv.at[rest], recv_sem).wait()
+    pltpu.make_async_copy(recv.at[rest, USED], recv.at[rest, USED], recv_sem).wait()
 
     for p in range(2):
         got = recv[p * CHAOS : (p + 1) * CHAOS].astype(F32).reshape(CHAOS * 8, WIDE).astype(BF16)
@@ -318,7 +323,7 @@
 
     for turn, p in enumerate(planes):
         half = 0.5 - p.astype(F32)
-        pltpu.make_async_copy(outer.at[p], outer.at[p], outer_recv_sem.at[p]).wait()
+        pltpu.make_async_copy(outer.at[p, :, USED], outer.at[p, :, USED], outer_recv_sem.at[p]).wait()
         beyond = dot(to_modes, outer[p].astype(F32).reshape(CHAOS * 8, WIDE).astype(BF16))
         rows = []
         for r in range(2):
@@ -335,8 +340,8 @@
 
         def give_back(hi, other):
             pltpu.make_async_remote_copy(
-                src_ref=back.at[hi, other],
-                dst_ref=home.at[me],
+                src_ref=back.at[hi, other, USED],
+                dst_ref=home.at[me, USED],
                 send_sem=back_send_sem,
                 recv_sem=back_recv_sem,
                 device_id=(2 * plane_pair + hi, other),
@@ -359,18 +364,18 @@
     collect = jnp.concatenate(collect, axis=1).astype(BF16)
 
     own_back.wait()
-    pltpu.make_async_copy(home.at[rest], home.at[rest], back_recv_sem).wait()
+    pltpu.make_async_copy(home.at[rest, USED], home.at[rest, USED], back_recv_sem).wait()
     got = home[...].astype(F32).reshape(GROUP * 8, WIDE).astype(BF16)
     result = dot(collect, got)
     for a in range(SLOT_DEV):
         for c in range(3):
             out_ref[a, c, 0] = result[a * 64 : (a + 1) * 64, c * LANES : (c + 1) * LANES].astype(BF16)
 
-    pltpu.make_async_copy(send.at[rest], send.at[rest], send_sem).wait()
-    pltpu.make_async_copy(send, send, outer_send_sem).wait()
+    pltpu.make_async_copy(send.at[rest, USED], send.at[rest, USED], send_sem).wait()
+    pltpu.make_async_copy(send.at[:, USED], send.at[:, USED], outer_send_sem).wait()
     for copy in halo_copies:
         copy.wait_send()
-    pltpu.make_async_copy(home.at[rest], home.at[rest], back_send_sem).wait()
+    pltpu.make_async_copy(home.at[rest, USED], home.at[rest, USED], back_send_sem).wait()
 
 
 def on_device(velocity, base_velocity, mode_slot, triples, triple_coef):

time: 25.5 us -> 24.5 us (0.961)
  Pallas kernels: 23.9 us -> 22.9 us
    pallas_call x1, Pallas kernels: 23.9 us -> 22.9 us  [on_device(): pl.pallas_call(functools.partial(kernel, space_count), out_shape=jax.Shap...]
where the time goes in v4:
time: 24.5 us; the launch traced here: 24.4 us
  Pallas kernels  22.9 us (93%)
  other arithmetic  0.87 us (4%)
  between operations  0.65 us (3%)
    pallas_call x1, Pallas kernels, on_device(): pl.pallas_call(functools.partial(kernel, space_count), out_shape=jax.Shap...  22.9 us
    sub x1, other arithmetic, on_device(): next_velocity = base_velocity - SECTION_STEP * convection  0.87 us

profile of v4, /device:TPU:1, one launch (start us, length us, event | category | flops | bytes accessed | tf_op | source)
XLA Modules:
  0.0 24.4 jit_solution(4289966296335514673)
XLA Ops:
  0.6 0.0 copy-start
  0.6 22.9 %shard_map.68 = bf16[3,3,1,64,128]{4,3,2,1,0:T(8,128)(2,1)S(1)} custom-call(f32[3,3,1,64,128]{4,3,2,1,0:T(8,128)} %velocity_ref.1, s32[1,35]{1,0:T(1,128)} %bitcast.5, s32[3,4096]{1,0:T(4,128)} %bitcast.3, bf16[4,8,128]{2,1,0:T(8,128)(2,1)} %bitcast.4), custom_call_target="tpu_custom_call" | custom-call | tf_op jit(solution)/shard_map/pallas_call | solution.py:391
  23.5 0.0 copy-done
  23.5 0.9 %multiply_subtract_fusion = (f32[3,3,1,64,128]{4,3,2,1,0:T(8,128)}, f32[3,3,1,64,128]{4,3,2,1,0:T(8,128)}) fusion(f32[3,3,1,64,128]{4,3,2,1,0:T(8,128)S(1)} %copy-done, bf16[3,3,1,64,128]{4,3,2,1,0:T(8,128)(2,1)S(1)} %shard_map.68), kind=kLoop, calls=%fused_computation | loop fusion | flops 221184 | bytes 1032192 | tf_op jit(solution)/shard_map/sub | solution.py:431
Async XLA Ops:
  0.6 22.9 %copy-start = (f32[3,3,1,64,128]{4,3,2,1,0:T(8,128)S(1)}, f32[3,3,1,64,128]{4,3,2,1,0:T(8,128)}, u32[]{:S(2)}) copy-start(f32[3,3,1,64,128]{4,3,2,1,0:T(8,128)} %param.6) | copy-start | bytes 884740

commit v5 on v4

--- a/solution.py
+++ b/solution.py
@@ -128,11 +128,13 @@
         lax.fori_loop(CHAOS // 2, CHAOS, go, 0, unroll=4)
         lax.fori_loop(turn, CHAOS // 2, go, 0, unroll=4 if turn == 0 else 7)
 
+    barrier = pltpu.get_barrier_semaphore()
+    toward = x_hi * z_up + (1 - x_hi) * z_down
+    away = x_hi * z_down + (1 - x_hi) * z_up
+    pl.semaphore_signal(barrier, inc=1, device_id=(2 * toward + x_hi, chaos), device_id_type=MESH)
+
     recv[...] = jnp.zeros(recv.shape, BF16)
     outer[...] = jnp.zeros(outer.shape, BF16)
-    home[...] = jnp.zeros(home.shape, BF16)
-
-    barrier = pltpu.get_barrier_semaphore()
 
     def greet(hi, other):
         pl.semaphore_signal(
@@ -141,9 +143,7 @@
 
     for turn in range(2):
         each_member(turn, greet)
-    toward = x_hi * z_up + (1 - x_hi) * z_down
-    away = x_hi * z_down + (1 - x_hi) * z_up
-    pl.semaphore_signal(barrier, inc=1, device_id=(2 * toward + x_hi, chaos), device_id_type=MESH)
+    home[...] = jnp.zeros(home.shape, BF16)
 
     row = iota((GROUP * 8, LANES), 0)
     source_row = ((row >> 1) & 3) * 64 + place_of(row >> 3) * 2 + (row & 1)

time: 24.5 us -> 24.1 us (0.984)
  Pallas kernels: 22.9 us -> 22.4 us
    pallas_call x1, Pallas kernels: 22.9 us -> 22.4 us  [on_device(): pl.pallas_call(functools.partial(kernel, space_count), out_shape=jax.Shap...]
where the time goes in v5:
time: 24.1 us; the launch traced here: 23.9 us
  Pallas kernels  22.4 us (93%)
  other arithmetic  0.87 us (4%)
  between operations  0.65 us (3%)
    pallas_call x1, Pallas kernels, on_device(): pl.pallas_call(functools.partial(kernel, space_count), out_shape=jax.Shap...  22.4 us
    sub x1, other arithmetic, on_device(): next_velocity = base_velocity - SECTION_STEP * convection  0.87 us

profile of v5, /device:TPU:1, one launch (start us, length us, event | category | flops | bytes accessed | tf_op | source)
XLA Modules:
  0.0 23.9 jit_solution(7544735137279474529)
XLA Ops:
  0.6 0.0 copy-start
  0.6 22.4 %shard_map.68 = bf16[3,3,1,64,128]{4,3,2,1,0:T(8,128)(2,1)S(1)} custom-call(f32[3,3,1,64,128]{4,3,2,1,0:T(8,128)} %velocity_ref.1, s32[1,35]{1,0:T(1,128)} %bitcast.5, s32[3,4096]{1,0:T(4,128)} %bitcast.3, bf16[4,8,128]{2,1,0:T(8,128)(2,1)} %bitcast.4), custom_call_target="tpu_custom_call" | custom-call | tf_op jit(solution)/shard_map/pallas_call | solution.py:391
  23.0 0.0 copy-done
  23.1 0.9 %multiply_subtract_fusion = (f32[3,3,1,64,128]{4,3,2,1,0:T(8,128)}, f32[3,3,1,64,128]{4,3,2,1,0:T(8,128)}) fusion(f32[3,3,1,64,128]{4,3,2,1,0:T(8,128)S(1)} %copy-done, bf16[3,3,1,64,128]{4,3,2,1,0:T(8,128)(2,1)S(1)} %shard_map.68), kind=kLoop, calls=%fused_computation | loop fusion | flops 221184 | bytes 1032192 | tf_op jit(solution)/shard_map/sub | solution.py:431
Async XLA Ops:
  0.6 22.4 %copy-start = (f32[3,3,1,64,128]{4,3,2,1,0:T(8,128)S(1)}, f32[3,3,1,64,128]{4,3,2,1,0:T(8,128)}, u32[]{:S(2)}) copy-start(f32[3,3,1,64,128]{4,3,2,1,0:T(8,128)} %param.6) | copy-start | bytes 884740
